TPU v7x, 512 devices: a whole 4x4x16 slice. The times are simulated.
512 devices in a mesh: dp: 64 (over z_lo, x, core), mp: 8 (over z_hi, y).
Axes of the slice: x: 4, y: 4, z: 16 (z_hi: 2, z_lo: 8; z = z_hi * 8 + z_lo), core: 2. Of those that a mesh axis runs over, the one named last changes fastest.
Arguments:
- inputs: bfloat16 [1024, 6144], P('dp', 'mp'), may hold values from -6 to 6
- targets: bfloat16 [1024, 6144], P('dp', 'mp'), may hold values from -6 to 6
- w_in: bfloat16 [6144, 16384], P('mp', 'dp'), may hold values from -6 to 6
- w_out: bfloat16 [16384, 6144], P('dp', 'mp'), may hold values from -6 to 6
- teach_in: float32 [6144, 16384], P('mp', 'dp'), may hold values from -6 to 6
- teach_out: float32 [16384, 6144], P('dp', 'mp'), may hold values from -6 to 6
Outputs:
- grad_in: bfloat16 [6144, 16384], P('mp', 'dp')
- grad_out: bfloat16 [16384, 6144], P('dp', 'mp')
- new_in: float32 [6144, 16384], P('mp', 'dp')
- new_out: float32 [16384, 6144], P('dp', 'mp')
All inputs are finite; a program needn't handle non-finite values.
Results may differ from a plain program's by a relative error of at most 0.017.
Values may be sent and summed in bfloat16 or wider, within the bound.
No kernel may reach another device: no remote copies, remote signals or barrier semaphores. Data moves between devices by JAX's collectives and lax.ppermute only.
A program may use at most 64 MiB of HBM per device.

v0:
```python
import math
import jax
import jax.numpy as jnp
from jax import lax
from jax.sharding import Mesh
from jax.sharding import PartitionSpec as P

D = 6144
FF = 16384
DP = ("dp_0", "dp_1", "dp_2")
decay_rate = 0.99
step_size = 0.5


def from_everyone(value, axis):
    copies = jnp.broadcast_to(value, (lax.axis_size(axis), *value.shape))
    return lax.all_to_all(copies, axis, split_axis=0, concat_axis=0, tiled=True)


def in_order(pieces, dim):
    pieces = jnp.moveaxis(pieces, 0, dim)
    dims = pieces.shape
    return pieces.reshape(*dims[:dim], dims[dim] * dims[dim + 1], *dims[dim + 2 :])


def gather_axes(value, axes, dim):
    far, near = axes
    pieces = from_everyone(from_everyone(value, far), near)
    return in_order(pieces.swapaxes(0, 1).reshape(-1, *value.shape), dim)


def cut_along(value, dim, size):
    before, after = (value.shape[:dim], value.shape[dim + 1 :])
    return jnp.moveaxis(value.reshape(*before, size, -1, *after), dim, 0)


def summed_on_arrival(value, axis, dim):
    pieces = cut_along(value, dim, lax.axis_size(axis))
    arrived = lax.all_to_all(pieces, axis, split_axis=0, concat_axis=0, tiled=True)
    return arrived.sum(axis=0)


def sum_in_two_steps(value, axes, dim):
    far, near = axes
    own = summed_on_arrival(cut_along(value, dim, lax.axis_size(far)), near, dim + 1)
    return jnp.sum(lax.all_to_all(own, far, 0, 0, tiled=True), axis=0)


def gelu_value(value):
    return 0.5 * value * (1.0 + jax.scipy.special.erf(value * (1.0 / math.sqrt(2.0))))


def gelu_slope(value):
    normal_cdf = 0.5 * (1.0 + jax.scipy.special.erf(value * (1.0 / math.sqrt(2.0))))
    return normal_cdf + value * jnp.exp(-0.5 * value * value) * (1.0 / math.sqrt(2.0 * math.pi))


def shards(inputs, targets, w_in, w_out, teach_in, teach_out):
    in_scale = 1.0 / math.sqrt(D)
    out_scale = 1.0 / math.sqrt(FF)
    gathered = gather_axes(inputs, (("dp_0", "dp_1"), "dp_2"), 0)
    partial_pre = jnp.dot(gathered, w_in, preferred_element_type=jnp.float32) * in_scale
    preact = lax.psum(partial_pre, "mp")
    hidden = gelu_value(preact).astype(jnp.bfloat16)
    block = hidden
    summed_rows = sum_in_two_steps(
        jnp.dot(block, w_out, preferred_element_type=jnp.float32) * out_scale,
        (("dp_0", "dp_1"), "dp_2"),
        0,
    )
    slope = (inputs.astype(jnp.float32) + summed_rows - targets.astype(jnp.float32)).astype(
        jnp.bfloat16
    )
    piece = gather_axes(slope, (("dp_0", "dp_1"), "dp_2"), 0)
    block = hidden
    grad_acc = jnp.einsum("tf,td->fd", block, piece, preferred_element_type=jnp.float32) * out_scale
    slope_part = (
        jnp.einsum("td,fd->tf", piece, w_out, preferred_element_type=jnp.float32) * out_scale
    )
    hidden_slope = lax.psum(slope_part.astype(jnp.bfloat16), "mp").astype(jnp.float32)
    pre_slope = (hidden_slope * gelu_slope(preact)).astype(jnp.bfloat16)
    grad_in = (
        jnp.einsum("td,tf->df", gathered, pre_slope, preferred_element_type=jnp.float32) * in_scale
    )
    new_in = decay_rate * teach_in + (1.0 - decay_rate) * (
        w_in.astype(jnp.float32) - step_size * grad_in
    )
    new_out = decay_rate * teach_out + (1.0 - decay_rate) * (
        w_out.astype(jnp.float32) - step_size * grad_acc
    )
    return (grad_in.astype(jnp.bfloat16), grad_acc.astype(jnp.bfloat16), new_in, new_out)


def solution(mesh):
    finer = Mesh(mesh.devices.reshape(8, 4, 2, mesh.shape["mp"]), ("dp_0", "dp_1", "dp_2", "mp"))
    return jax.shard_map(
        shards,
        mesh=finer,
        in_specs=(P(DP, "mp"), P(DP, "mp"), P("mp", DP), P(DP, "mp"), P("mp", DP), P(DP, "mp")),
        out_specs=(P("mp", DP), P(DP, "mp"), P("mp", DP), P(DP, "mp")),
        check_vma=False,
    )
```

profile of v0, /device:TPU:2, one launch (start us, length us, event | category | flops | bytes accessed | tf_op | source)
XLA Modules:
  0.0 558.3 jit_solution(2530100006321149228)
XLA Ops:
  7.2 0.0 all-reduce.3.cloned.1.call-start
  7.2 0.8 broadcast_in_dim.12
  8.0 54.8 %all_to_all.30 = bf16[32,16,768]{2,1,0:T(8,128)(2,1)S(1)} all-to-all(bf16[32,16,768]{2,1,0:T(8,128)(2,1)S(1)} %broadcast_in_dim.12), channel_id=1, replica_groups=mesh['dp_0'=8,'dp_1'=4,'dp_2'=2,'mp'=8] {'dp_0','dp_1'}, dimensions={0} | all-to-all | bytes 1572864 | tf_op jit(solution)/shard_map/all_to_all | solution.py:17
  62.8 0.1 broadcast_in_dim.13
  62.9 5.0 all_to_all.31
  67.9 0.0 copy-start.1
  67.9 0.2 copy.25
  68.1 0.8 copy-done.1
  68.9 1.6 convolution_multiply_fusion.2
  70.5 0.0 copy-start.2
  70.5 0.0 all-reduce.3.cloned.1.call-update
  70.5 0.0 all-reduce.5.cloned.1.call-start
  70.5 172.3 %all-reduce.3.cloned.1.call-done = f32[1024,256]{1,0:T(8,128)} async-done(((f32[1024,256]{1,0:T(8,128)}), f32[1024,256]{1,0:T(8,128)}) %all-reduce.3.cloned.1.call-update) | async-done | bytes 1048592 | tf_op jit(solution)/shard_map/psum | solution.py:63
  242.8 1.4 multiply_convert_fusion
  244.2 0.0 copy-done.2
  244.2 0.0 copy-start
  244.2 0.6 convolution_multiply_fusion
  244.8 0.2 copy-done
  245.0 0.2 copy.33
  245.3 7.2 %all_to_all.32 = f32[2,32,16,768]{3,2,1,0:T(8,128)} all-to-all(f32[2,32,16,768]{3,2,1,0:T(8,128)S(1)} %bitcast.29), channel_id=1, replica_groups=mesh['dp_0'=8,'dp_1'=4,'dp_2'=2,'mp'=8] {'dp_2'}, dimensions={0} | all-to-all | bytes 6291456 | tf_op jit(solution)/shard_map/all_to_all | solution.py:39
  252.5 3.4 reduce_sum.18
  255.9 88.0 %all_to_all.33 = f32[32,16,768]{2,1,0:T(8,128)S(1)} all-to-all(f32[32,16,768]{2,1,0:T(8,128)} %reduce_sum.18), channel_id=1, replica_groups=mesh['dp_0'=8,'dp_1'=4,'dp_2'=2,'mp'=8] {'dp_0','dp_1'}, dimensions={0} | all-to-all | bytes 3145728 | tf_op jit(solution)/shard_map/all_to_all | solution.py:46
  343.9 0.7 reduce_sum.19
  344.6 0.8 subtract_convert_fusion
  345.4 0.1 broadcast_in_dim.14
  345.5 46.4 %all_to_all.34 = bf16[32,16,768]{2,1,0:T(8,128)(2,1)S(1)} all-to-all(bf16[32,16,768]{2,1,0:T(8,128)(2,1)S(1)} %broadcast_in_dim.14), channel_id=1, replica_groups=mesh['dp_0'=8,'dp_1'=4,'dp_2'=2,'mp'=8] {'dp_0','dp_1'}, dimensions={0} | all-to-all | bytes 1572864 | tf_op jit(solution)/shard_map/all_to_all | solution.py:17
  391.9 0.1 broadcast_in_dim.15
  392.0 5.0 all_to_all.35
  397.0 0.2 copy.27
  397.2 1.4 fusion
  398.6 0.0 all-reduce.5.cloned.1.call-update
  398.6 1.2 copy.29
  399.8 2.3 copy.28
  402.1 3.1 multiply_add_fusion
  405.2 141.6 %all-reduce.5.cloned.1.call-done = bf16[1024,256]{1,0:T(8,128)(2,1)} async-done(((bf16[1024,256]{1,0:T(8,128)(2,1)}), bf16[1024,256]{1,0:T(8,128)(2,1)}) %all-reduce.5.cloned.1.call-update) | async-done | bytes 524304 | tf_op jit(solution)/shard_map/psum | solution.py:80
  546.8 2.4 fusion.8
  549.3 0.1 fusion.14
  549.4 0.9 copy.30
  550.3 1.1 copy.31
Async XLA Ops:
  7.2 235.6 %all-reduce.3.cloned.1.call-start = ((), (), s32[]{:S(2)}) async-start(), calls=%async_computation.6 | async-start | bytes 2097152 | tf_op jit(solution)/shard_map/psum | solution.py:63
  67.9 1.0 copy-start.1
  70.5 173.8 %copy-start.2 = (bf16[256,768]{1,0:T(8,128)(2,1)S(1)}, bf16[256,768]{1,0:T(8,128)(2,1)}, u32[]{:S(2)}) copy-start(bf16[256,768]{1,0:T(8,128)(2,1)} %param.9) | copy-start | bytes 1179652
  70.5 476.3 %all-reduce.5.cloned.1.call-start = ((), (), s32[]{:S(2)}) async-start(), calls=%async_computation.7 | async-start | bytes 1048576 | tf_op jit(solution)/shard_map/psum | solution.py:80
  244.2 0.8 copy-start
Sparse Core Ops, SparseCore 0:
  70.6 172.1 all-reduce.2
  398.8 148.0 all-reduce.4
where the time goes:
time: 559 us; the launch traced here: 558 us
  waiting for transfers between devices  314 us (56%)
  blocking collectives  206 us (37%)
  between operations  14.1 us (3%)
  matrix products  9.11 us (2%)
  local copies, waits for them, and re-layouts  8.2 us (1%)
  other arithmetic  6.41 us (1%)
    psum x1, waiting for transfers between devices, shards(): preact = lax.psum(partial_pre, 'mp')  172 us
    psum x1, waiting for transfers between devices, shards(): lax.psum(slope_part.astype(jnp.bfloat16), 'mp').astype(jnp.float32)  142 us
    all_to_all x4, blocking collectives, from_everyone(): return lax.all_to_all(copies, axis, split_axis=0, concat_axis=0, tiled=True)  111 us
    all_to_all x1, blocking collectives, sum_in_two_steps(): return jnp.sum(lax.all_to_all(own, far, 0, 0, tiled=True), axis=0)  88 us
  transfers between devices with their start and end apart: 2, of which 2 were waited for; matrix products, arithmetic and copies ran while one was open for 1% of the time, Pallas kernels for 0%

commit v1 on v0

--- a/solution.py
+++ b/solution.py
@@ -60,7 +60,7 @@
     out_scale = 1.0 / math.sqrt(FF)
     gathered = gather_axes(inputs, (("dp_0", "dp_1"), "dp_2"), 0)
     partial_pre = jnp.dot(gathered, w_in, preferred_element_type=jnp.float32) * in_scale
-    preact = lax.psum(partial_pre, "mp")
+    preact = jnp.sum(lax.all_gather(partial_pre, "mp"), axis=0)
     hidden = gelu_value(preact).astype(jnp.bfloat16)
     block = hidden
     summed_rows = sum_in_two_steps(

time: 559 us -> 684 us (1.22)
  waiting for transfers between devices: 314 us -> 422 us
  blocking collectives: 206 us -> 217 us
    all_gather x0 -> x1, waiting for transfers between devices: none -> 280 us  [shards(): preact = jnp.sum(lax.all_gather(partial_pre, 'mp'), axis=0)]
    psum x1 -> x0, waiting for transfers between devices: 172 us -> none  [shards(): preact = lax.psum(partial_pre, 'mp')]
    all_to_all x1, blocking collectives: 88 us -> 98.8 us  [sum_in_two_steps(): return jnp.sum(lax.all_to_all(own, far, 0, 0, tiled=True), axis=0)]
where the time goes in v1:
time: 684 us; the launch traced here: 683 us
  waiting for transfers between devices  422 us (62%)
  blocking collectives  217 us (32%)
  between operations  14.1 us (2%)
  other arithmetic  10.7 us (2%)
  local copies, waits for them, and re-layouts  9.75 us (1%)
  matrix products  9.12 us (1%)
    all_gather x1, waiting for transfers between devices, shards(): preact = jnp.sum(lax.all_gather(partial_pre, 'mp'), axis=0)  280 us
    psum x1, waiting for transfers between devices, shards(): lax.psum(slope_part.astype(jnp.bfloat16), 'mp').astype(jnp.float32)  142 us
    all_to_all x4, blocking collectives, from_everyone(): return lax.all_to_all(copies, axis, split_axis=0, concat_axis=0, tiled=True)  111 us
    all_to_all x1, blocking collectives, sum_in_two_steps(): return jnp.sum(lax.all_to_all(own, far, 0, 0, tiled=True), axis=0)  98.8 us
  transfers between devices with their start and end apart: 2, of which 2 were waited for; matrix products, arithmetic and copies ran while one was open for 1% of the time, Pallas kernels for 0%

profile of v1, /device:TPU:2, one launch (start us, length us, event | category | flops | bytes accessed | tf_op | source)
XLA Modules:
  0.0 683.4 jit_solution(14006469738494107793)
XLA Ops:
  7.2 0.0 all-gather.3.cloned.1.call-start
  7.2 0.8 broadcast_in_dim.12
  8.0 54.8 %all_to_all.30 = bf16[32,16,768]{2,1,0:T(8,128)(2,1)S(1)} all-to-all(bf16[32,16,768]{2,1,0:T(8,128)(2,1)S(1)} %broadcast_in_dim.12), channel_id=1, replica_groups=mesh['dp_0'=8,'dp_1'=4,'dp_2'=2,'mp'=8] {'dp_0','dp_1'}, dimensions={0} | all-to-all | bytes 1572864 | tf_op jit(solution)/shard_map/all_to_all | solution.py:17
  62.8 0.1 broadcast_in_dim.13
  62.9 5.0 all_to_all.31
  67.9 0.0 copy-start.1
  67.9 0.2 copy.25
  68.1 0.8 copy-done.1
  68.9 1.6 convolution_multiply_fusion.2
  70.5 0.0 all-gather.3.cloned.1.call-update
  70.5 0.0 all-reduce.2.cloned.1.call-start
  70.6 279.9 %all-gather.3.cloned.1.call-done = f32[8192,256]{1,0:T(8,128)} async-done(((f32[1024,256]{1,0:T(8,128)}), f32[8192,256]{1,0:T(8,128)}) %all-gather.3.cloned.1.call-update) | async-done | bytes 8388624 | tf_op jit(solution)/shard_map/all_gather | solution.py:63
  350.5 4.1 reduce_sum.27
  354.5 0.0 copy-start.2
  354.5 0.2 multiply_convert_fusion
  354.7 0.8 copy-done.2
  355.5 0.6 convolution_multiply_fusion
  356.1 0.2 copy.33
  356.3 7.2 %all_to_all.32 = f32[2,32,16,768]{3,2,1,0:T(8,128)} all-to-all(f32[2,32,16,768]{3,2,1,0:T(8,128)S(1)} %bitcast.30), channel_id=1, replica_groups=mesh['dp_0'=8,'dp_1'=4,'dp_2'=2,'mp'=8] {'dp_2'}, dimensions={0} | all-to-all | bytes 6291456 | tf_op jit(solution)/shard_map/all_to_all | solution.py:39
  363.6 3.4 reduce_sum.28
  367.0 98.8 %all_to_all.33 = f32[32,16,768]{2,1,0:T(8,128)} all-to-all(f32[32,16,768]{2,1,0:T(8,128)} %reduce_sum.28), channel_id=1, replica_groups=mesh['dp_0'=8,'dp_1'=4,'dp_2'=2,'mp'=8] {'dp_0','dp_1'}, dimensions={0} | all-to-all | bytes 3145728 | tf_op jit(solution)/shard_map/all_to_all | solution.py:46
  465.8 2.1 reduce_sum.29
  467.9 0.8 subtract_convert_fusion
  468.7 0.1 broadcast_in_dim.14
  468.8 46.4 %all_to_all.34 = bf16[32,16,768]{2,1,0:T(8,128)(2,1)S(1)} all-to-all(bf16[32,16,768]{2,1,0:T(8,128)(2,1)S(1)} %broadcast_in_dim.14), channel_id=1, replica_groups=mesh['dp_0'=8,'dp_1'=4,'dp_2'=2,'mp'=8] {'dp_0','dp_1'}, dimensions={0} | all-to-all | bytes 1572864 | tf_op jit(solution)/shard_map/all_to_all | solution.py:17
  515.2 0.1 broadcast_in_dim.15
  515.3 5.0 all_to_all.35
  520.3 0.0 copy-start.3
  520.3 0.2 copy.27
  520.5 0.0 copy-start
  520.6 1.2 copy-done
  521.7 0.0 copy-done.3
  521.7 1.4 fusion
  523.1 0.0 all-reduce.2.cloned.1.call-update
  523.1 0.9 copy.29
  524.1 0.0 copy-start.4
  524.1 2.3 copy.28
  526.4 0.0 copy-done.4
  526.4 3.3 multiply_add_fusion
  529.7 142.5 %all-reduce.2.cloned.1.call-done = bf16[1024,256]{1,0:T(8,128)(2,1)} async-done(((bf16[1024,256]{1,0:T(8,128)(2,1)}), bf16[1024,256]{1,0:T(8,128)(2,1)}) %all-reduce.2.cloned.1.call-update) | async-done | bytes 524304 | tf_op jit(solution)/shard_map/psum | solution.py:80
  672.2 2.2 fusion.8
  674.4 0.1 fusion.14
  674.5 0.9 copy.30
  675.4 1.1 copy.31
Async XLA Ops:
  7.2 343.3 %all-gather.3.cloned.1.call-start = ((), (), s32[]{:S(2)}) async-start(), calls=%async_computation.7 | async-start | bytes 9437184 | tf_op jit(solution)/shard_map/all_gather | solution.py:63
  67.9 1.0 copy-start.1
  70.5 601.6 %all-reduce.2.cloned.1.call-start = ((), (), s32[]{:S(2)}) async-start(), calls=%async_computation.6 | async-start | bytes 1048576 | tf_op jit(solution)/shard_map/psum | solution.py:80
  354.5 1.0 copy-start.2
  520.3 1.4 copy-start.3
  520.5 1.2 copy-start
  524.1 2.3 copy-start.4
Sparse Core Ops, SparseCore 0:
  70.7 279.7 all-gather.2
  523.3 148.8 all-reduce.1
